TPU v7x, 256 devices: a whole 4x4x8 slice. The times are simulated.
256 devices in a mesh: ctx: 32 (over z, x), head: 4 (over y_hi, core), side: 2 (over y_lo).
Axes of the slice: x: 4, y: 4 (y_hi: 2, y_lo: 2; y = y_hi * 2 + y_lo), z: 8, core: 2. Of those that a mesh axis runs over, the one named last changes fastest.
Arguments:
- prefill_query: bfloat16 [8192, 64, 128], P('ctx', ('head', 'side')), may hold values from -6 to 6
- prefill_keys: bfloat16 [8192, 8, 128], P('ctx', ('head', 'side')), may hold values from -6 to 6
- prefill_values: bfloat16 [8192, 8, 128], P('ctx', ('head', 'side')), may hold values from -6 to 6
- token_pos: int32 [8192], P('ctx'), may hold values from 0 to 8191, as said below
- scale_exp: int32 [1024, 8, 2], P('ctx', ('head', 'side')), may hold values from -7 to -5
- page_owner: int32 [1024], P('ctx'), may hold values from 0 to 31, as said below
- draft_query: bfloat16 [256, 64, 128], P(None, ('head', 'side')), may hold values from -6 to 6
- draft_keys: bfloat16 [256, 8, 128], P('side', 'head'), may hold values from -6 to 6
- draft_values: bfloat16 [256, 8, 128], P('side', 'head'), may hold values from -6 to 6
- parents: int32 [256], replicated, may hold values from 0 to 254, as said below
Outputs:
- prefill_out: bfloat16 [8192, 64, 128], P('ctx', ('head', 'side'))
- cache_keys: bfloat16 [8192, 8, 128], P('ctx', ('head', 'side'))
- cache_values: bfloat16 [8192, 8, 128], P('ctx', ('head', 'side'))
- verify_out: bfloat16 [256, 64, 128], P('ctx', ('head', 'side'))
Inputs may be any that keep to these rules, and one draw needn't show every extreme that they name: `token_pos`: a permutation of 0 to 8191; the rows of shard c of ctx hold the runs a and 2 * 32 - 1 - a of 128 consecutive positions, in order, with a different a for each shard. `page_owner`: the 1024 // 32 entries of one ctx shard are a permutation of 0 to 32 - 1. parents[0] = 0, and parents[r] < r for r >= 1.
All inputs are finite; a program needn't handle non-finite values.
Results may differ from a plain program's by a relative error of at most 0.0049.
Values may be sent and summed in bfloat16 or wider, within the bound.
No kernel may reach another device: no remote copies, remote signals or barrier semaphores. Data moves between devices by JAX's collectives and lax.ppermute only.
A program may use at most 64 MiB of HBM per device.

v0:
```python
import math
import jax
import jax.numpy as jnp
import numpy as np
from jax import lax
from jax.sharding import Mesh
from jax.sharding import PartitionSpec as P

CTX = ("ctx_0", "ctx_1")
NEG_FILL = -1e30
FP_LIMIT = 448.0
LOG_TWO_E = 1.4426950408889634


def side_by_side(arrays, axis, dim, along):
    widths = [a.shape[along] for a in arrays]
    both = jnp.concatenate(arrays, axis=along)
    whole = lax.all_gather(both, axis, axis=dim, tiled=True)
    return tuple(jnp.split(whole, [sum(widths[:k]) for k in range(1, len(widths))], axis=along))


def sent_together(arrays, axis, split_dim, concat_dim, along):
    columns = [a.reshape(*a.shape[:along], -1) for a in arrays]
    both = jnp.concatenate(columns, axis=along)
    whole, at, outs = (
        lax.all_to_all(both, axis, split_axis=split_dim, concat_axis=concat_dim, tiled=True),
        0,
        [],
    )
    for a, column in zip(arrays, columns):
        section = whole[..., at : at + column.shape[along]]
        outs.append(section.reshape(*section.shape[:along], *a.shape[along:]))
        at += column.shape[along]
    return tuple(outs)


def sent_together_2(arrays, axis, split_dim, concat_dim, along):
    ends, at = ([], 0)
    for a in arrays[:-1]:
        at += a.shape[along]
        ends.append(at)
    both = jnp.concatenate(arrays, axis=along)
    return tuple(
        jnp.split(
            lax.all_to_all(both, axis, split_axis=split_dim, concat_axis=concat_dim, tiled=True),
            ends,
            axis=along,
        )
    )


def sent_to_all(array, axis):
    devices = lax.axis_size(axis)
    return lax.all_to_all(
        jnp.broadcast_to(array[None], (devices, *array.shape)), axis, 0, 0, tiled=True
    )


def taken_together(array, axis):
    everything = sent_to_all(array, axis)
    return jnp.max(everything, axis=0)


def summed_rows(array, axes, dim):
    if not axes:
        return array
    nearer = lax.psum_scatter(array, axes[0], scatter_dimension=dim, tiled=True)
    return summed_rows(nearer, axes[1:], dim)


def power_two(exponent):
    levels = jnp.arange(-7, -4, dtype=jnp.int32)
    table = jnp.asarray(np.array([2.0**level for level in range(-7, -4)], np.float32))
    return jnp.sum(jnp.where(exponent[..., None] == levels, table, jnp.float32(0.0)), axis=-1)


def ancestors(parent_rows):
    row_total = parent_rows.shape[0]
    row_index = jnp.arange(row_total, dtype=jnp.int32)
    linked = (
        (parent_rows[:, None] == row_index[None, :]) | (row_index[:, None] == row_index[None, :])
    ).astype(jnp.float32)
    for _ in range(row_total.bit_length()):
        linked = jnp.minimum(
            jnp.dot(linked, linked, precision=lax.Precision.HIGHEST), jnp.float32(1.0)
        )
    return linked > 0.5


def online_step(running, scores, allowed, value_block):
    old_top, old_mass, old_numer = running
    block_top = jnp.ceil(LOG_TWO_E * jnp.max(jnp.where(allowed, scores, NEG_FILL), axis=1))
    new_top = jnp.maximum(old_top, block_top)
    weights = jnp.where(allowed, jnp.exp2(LOG_TWO_E * scores - new_top[:, None]), jnp.float32(0.0))
    factor = jnp.exp2(old_top - new_top)
    new_mass = old_mass * factor + jnp.sum(weights, axis=1)
    new_numer = old_numer * factor[:, None] + jnp.dot(
        weights.astype(jnp.bfloat16), value_block, preferred_element_type=jnp.float32
    )
    return (new_top, new_mass, new_numer)


def body(
    prefill_query,
    prefill_keys,
    prefill_values,
    token_pos,
    scale_exp,
    page_owner,
    draft_query,
    draft_keys,
    draft_values,
    parents,
):
    tok_rows, groups, width = prefill_query.shape
    scale_factor = width ** (-0.5)
    shard_total = lax.axis_size(CTX)
    page_rows = tok_rows // shard_total
    my_index = lax.axis_index(CTX)
    query_rows = prefill_query.reshape(tok_rows * groups, width)
    query_places = jnp.repeat(token_pos, groups)
    local_keys = prefill_keys.reshape(tok_rows, width)
    local_values = prefill_values.reshape(tok_rows, width)
    page_scales = power_two(scale_exp.reshape(shard_total, 2))
    start_state = (
        jnp.full((tok_rows * groups,), NEG_FILL, jnp.float32),
        jnp.zeros((tok_rows * groups,), jnp.float32),
        jnp.zeros((tok_rows * groups, width), jnp.float32),
    )

    def attend(running, key_block, value_block, place_block):
        scores = scale_factor * jnp.einsum(
            "qd,kd->qk", query_rows, key_block, preferred_element_type=jnp.float32
        )
        allowed = query_places[:, None] >= place_block[None, :]
        return online_step(running, scores, allowed, value_block)

    running = start_state
    key_piece, value_piece, place_piece = (
        *side_by_side((local_keys, local_values), CTX, 0, 1),
        lax.all_gather(token_pos, CTX, axis=0, tiled=True),
    )
    row_count = key_piece.shape[0]
    block_rows = math.gcd(row_count, 512)
    block_total = row_count // block_rows

    def inner_rows(carry_in, item):
        return (attend(carry_in, item[0], item[1], item[2]), None)

    running, _ = lax.scan(
        inner_rows,
        running,
        (
            key_piece.reshape(block_total, block_rows, width),
            value_piece.reshape(block_total, block_rows, width),
            place_piece.reshape(block_total, block_rows),
        ),
    )
    paged_keys = local_keys.reshape(shard_total, page_rows, width).astype(jnp.float32)
    paged_values = local_values.reshape(shard_total, page_rows, width).astype(jnp.float32)
    scaled_keys = jnp.clip(paged_keys / page_scales[:, 0, None, None], -FP_LIMIT, FP_LIMIT).astype(
        jnp.bfloat16
    )
    scaled_values = jnp.clip(
        paged_values / page_scales[:, 1, None, None], -FP_LIMIT, FP_LIMIT
    ).astype(jnp.bfloat16)
    slot_index = jnp.arange(shard_total, dtype=jnp.int32)
    inverse = jnp.sum(
        jnp.where(page_owner[None, :] == slot_index[:, None], slot_index[None, :], 0), axis=1
    )
    got_keys, got_values, got_scales = sent_together(
        (
            jnp.take(scaled_keys, inverse, axis=0),
            jnp.take(scaled_values, inverse, axis=0),
            jnp.take(page_scales, inverse, axis=0).astype(jnp.bfloat16),
        ),
        CTX,
        0,
        0,
        1,
    )
    scale_back = got_scales.astype(jnp.float32)
    cache_keys = (
        (got_keys.astype(jnp.float32) * scale_back[:, 0, None, None])
        .astype(jnp.bfloat16)
        .reshape(tok_rows, width)
    )
    cache_values = (
        (got_values.astype(jnp.float32) * scale_back[:, 1, None, None])
        .astype(jnp.bfloat16)
        .reshape(tok_rows, width)
    )
    prefill_out = (
        (running[2] / running[1][:, None]).astype(jnp.bfloat16).reshape(tok_rows, groups, width)
    )
    tree_keys, tree_values = sent_together_2((draft_keys, draft_values), "side", 1, 0, 2)
    row_total = draft_query.shape[0]
    tree_keys = tree_keys.reshape(row_total, width)
    tree_values = tree_values.reshape(row_total, width)
    draft_rows = draft_query.reshape(row_total * groups, width)
    cache_scores = scale_factor * jnp.einsum(
        "qd,kd->qk", draft_rows, cache_keys, preferred_element_type=jnp.float32
    )
    cache_top = jnp.ceil(LOG_TWO_E * jnp.max(cache_scores, axis=1))
    tree_mask = jnp.repeat(ancestors(parents), groups, axis=0)
    tree_scores = scale_factor * jnp.einsum(
        "qd,kd->qk", draft_rows, tree_keys, preferred_element_type=jnp.float32
    )
    tree_top = jnp.ceil(LOG_TWO_E * jnp.max(jnp.where(tree_mask, tree_scores, NEG_FILL), axis=1))
    tree_weights = jnp.where(
        tree_mask, jnp.exp2(LOG_TWO_E * tree_scores - tree_top[:, None]), jnp.float32(0.0)
    )
    tree_mass = jnp.sum(tree_weights, axis=1)
    tree_numer = jnp.dot(
        tree_weights.astype(jnp.bfloat16), tree_values, preferred_element_type=jnp.float32
    )
    share_rows = row_total // shard_total

    def own_rows(array):
        return lax.dynamic_slice_in_dim(array, my_index * share_rows, share_rows, 0)

    global_top = taken_together(cache_top, CTX)
    cache_weights = jnp.exp2(LOG_TWO_E * cache_scores - global_top[:, None])
    cache_mass = jnp.sum(cache_weights, axis=1).reshape(row_total, groups)
    cache_numer = jnp.dot(
        cache_weights.astype(jnp.bfloat16), cache_values, preferred_element_type=jnp.float32
    ).reshape(row_total, groups, width)
    far_mass, far_numer = (summed_rows(cache_mass, CTX, 0), summed_rows(cache_numer, CTX, 0))
    far_top = own_rows(global_top.reshape(row_total, groups))
    near_top = own_rows(tree_top.reshape(row_total, groups))
    near_mass = own_rows(tree_mass.reshape(row_total, groups))
    near_numer = own_rows(tree_numer.reshape(row_total, groups, width))
    joint_top = jnp.maximum(far_top, near_top)
    far_factor = jnp.exp2(far_top - joint_top)
    near_factor = jnp.exp2(near_top - joint_top)
    numer_total = far_numer * far_factor[..., None] + near_numer * near_factor[..., None]
    mass_total = far_mass * far_factor + near_mass * near_factor
    verify_out = (numer_total / mass_total[..., None]).astype(jnp.bfloat16)
    return (
        prefill_out,
        cache_keys.reshape(tok_rows, 1, width),
        cache_values.reshape(tok_rows, 1, width),
        verify_out,
    )


def solution(mesh):
    finer = Mesh(
        mesh.devices.reshape(8, 4, mesh.shape["head"], mesh.shape["side"]),
        ("ctx_0", "ctx_1", "head", "side"),
    )
    in_specs = (
        P(CTX, ("head", "side"), None),
        P(CTX, ("head", "side"), None),
        P(CTX, ("head", "side"), None),
        P(CTX),
        P(CTX, ("head", "side"), None),
        P(CTX),
        P(None, ("head", "side"), None),
        P("side", "head", None),
        P("side", "head", None),
        P(),
    )
    out_specs = (
        P(CTX, ("head", "side"), None),
        P(CTX, ("head", "side"), None),
        P(CTX, ("head", "side"), None),
        P(CTX, ("head", "side"), None),
    )
    return jax.shard_map(body, mesh=finer, in_specs=in_specs, out_specs=out_specs, check_vma=False)
```

profile of v0, /device:TPU:8, one launch (start us, length us, event | category | flops | bytes accessed | tf_op | source)
XLA Modules:
  0.0 365.7 jit_solution(1240601794977269774)
XLA Ops:
  14.2 21.9 %all_to_all.36 = bf16[32,2,1025]{2,1,0:T(2,128)(2,1)S(1)} all-to-all(bf16[32,2,1025]{2,1,0:T(2,128)(2,1)S(1)} %reshape.283), channel_id=1, replica_groups=mesh['ctx_0'=8,'ctx_1'=4,'head'=4,'side'=2] {'ctx_0','ctx_1'}, dimensions={0} | all-to-all | bytes 262400 | tf_op jit(solution)/shard_map/all_to_all | solution.py:26
  37.9 3.9 %all-to-all-start.1 = ((f32[32,1,2048]{2,1,0:T(1,128)}), f32[32,1,2048]{2,1,0:T(1,128)S(1)}, u32[]{:S(2)}, u32[]{:S(2)}) async-start(f32[32,1,2048]{2,1,0:T(1,128)} %broadcast_in_dim.109), calls=%async_computation.1 | async-start | bytes 524288 | tf_op jit(solution)/shard_map/all_to_all | solution.py:54
  41.9 11.8 %all-to-all-done.1 = f32[32,1,2048]{2,1,0:T(1,128)S(1)} async-done(((f32[32,1,2048]{2,1,0:T(1,128)}), f32[32,1,2048]{2,1,0:T(1,128)S(1)}, u32[]{:S(2)}, u32[]{:S(2)}) %all-to-all-start.1) | async-done | bytes 262176 | tf_op jit(solution)/shard_map/all_to_all | solution.py:54
  59.2 33.4 %reduce-scatter.4.cloned.1.call-done = f32[32,8,128]{2,0,1:T(8,128)} async-done(((f32[256,8,128]{2,0,1:T(8,128)}), f32[32,8,128]{2,0,1:T(8,128)}) %reduce-scatter.4.cloned.1.call-update) | async-done | bytes 131088 | tf_op jit(solution)/shard_map/reduce_scatter | solution.py:67
  94.2 3.9 %all-to-all-start.2 = ((bf16[128,2,256]{2,0,1:T(8,128)(2,1)}), bf16[128,2,256]{2,0,1:T(8,128)(2,1)S(1)}, u32[]{:S(2)}, u32[]{:S(2)}) async-start(bf16[128,2,256]{2,0,1:T(8,128)(2,1)} %pad_maximum_fusion.1), calls=%async_computation.4 | async-start | bytes 262144 | tf_op jit(solution)/shard_map/all_to_all | solution.py:45
  101.8 42.4 %all-gather = s32[32,1,256]{2,1,0:T(1,128)S(1)} all-gather(s32[1,1,256]{2,1,0:T(1,128)S(1)} %bitcast.145), channel_id=1, replica_groups=mesh['ctx_0'=8,'ctx_1'=4,'head'=4,'side'=2] {'ctx_0','ctx_1'}, dimensions={0}, use_global_device_ids=true | all-gather | bytes 33792 | tf_op jit(solution)/shard_map/all_gather | solution.py:141
  153.2 16.3 %all-reduce = f32[32,8]{1,0:T(8,128)S(1)} all-reduce(f32[32,8]{1,0:T(8,128)} %reduce-scatter.8.cloned.1.call-done), channel_id=5, replica_groups=mesh['ctx_0'=8,'ctx_1'=4,'head'=4,'side'=2] {'ctx_1'}, use_global_device_ids=true, to_apply=%region_13.15.clone | all-reduce | flops 256 | bytes 2048
  171.9 5.0 %all-gather.3.cloned.1.call-done = bf16[8192,256]{1,0:T(8,128)(2,1)} async-done(((bf16[256,256]{1,0:T(8,128)(2,1)}), bf16[8192,256]{1,0:T(8,128)(2,1)}) %all-gather.3.cloned.1.call-update) | async-done | bytes 4194320 | tf_op jit(solution)/shard_map/all_gather | solution.py:18
  176.9 3.8 %fusion.54 = (bf16[8192,128]{1,0:T(8,128)(2,1)S(1)}, bf16[8192,128]{1,0:T(8,128)(2,1)}) fusion(bf16[8192,256]{1,0:T(8,128)(2,1)} %all-gather.3.cloned.1.call-done), kind=kLoop, calls=%fused_computation.116 | loop fusion | bytes 8388608 | tf_op jit(solution)/shard_map/split | solution.py:19
  180.7 175.6 %while.17 = (s32[]{:T(128)}, f32[2048]{0:T(1024)S(1)}, f32[2048]{0:T(1024)S(1)}, f32[2048,128]{1,0:T(8,128)}, s32[16,512]{1,0:T(8,128)S(1)}, /*index=5*/bf16[16,...) while((s32[]{:T(128)}, f32[2048]{0:T(1024)S(1)}, ...), condition=%wide.region_3.4_spmd.clone, body=%wide.region_0.3_spmd.clone.sunk | while | flops 554450944 | bytes 32435368 | solution.py:150
  197.8 3.7 %convolution_add_fusion.2 = f32[2048,128]{1,0:T(8,128)} fusion(f32[512,2048]{1,0:T(8,128)S(1)} %copy-done.1, f32[2048]{0:T(1024)S(1)} %ceil_maximum_fusion.2, s32[2048]{0:T(1024)S(1)} %ge.96, s32[512]{0:T(512)S(1)} %bitcast.144, f32[2048,128]{1,0:T(8,128)} %get-tuple-element.306, f32[2048]{0:T(1024)S(1)} %get-tuple-element.291, pred[]{:T(512)S(6)} %compare.3, ...), kind=kOutput, calls=%fused_computation.9.clone.1 | convolution fusion | flops 275513344 | bytes 6449157 | tf_op jit(solution)/shard_map/while/body/eval_jaxpr/dot_general | solution.py:97
  208.9 3.7 %convolution_add_fusion.2 = f32[2048,128]{1,0:T(8,128)} fusion(f32[512,2048]{1,0:T(8,128)S(1)} %copy-done.1, f32[2048]{0:T(1024)S(1)} %ceil_maximum_fusion.2, s32[2048]{0:T(1024)S(1)} %ge.96, s32[512]{0:T(512)S(1)} %bitcast.144, f32[2048,128]{1,0:T(8,128)} %get-tuple-element.306, f32[2048]{0:T(1024)S(1)} %get-tuple-element.291, pred[]{:T(512)S(6)} %compare.3, ...), kind=kOutput, calls=%fused_computation.9.clone.1 | convolution fusion | flops 275513344 | bytes 6449157 | tf_op jit(solution)/shard_map/while/body/eval_jaxpr/dot_general | solution.py:97
  212.8 3.6 fusion.83
  219.9 3.7 %convolution_add_fusion.2 = f32[2048,128]{1,0:T(8,128)} fusion(f32[512,2048]{1,0:T(8,128)S(1)} %copy-done.1, f32[2048]{0:T(1024)S(1)} %ceil_maximum_fusion.2, s32[2048]{0:T(1024)S(1)} %ge.96, s32[512]{0:T(512)S(1)} %bitcast.144, f32[2048,128]{1,0:T(8,128)} %get-tuple-element.306, f32[2048]{0:T(1024)S(1)} %get-tuple-element.291, pred[]{:T(512)S(6)} %compare.3, ...), kind=kOutput, calls=%fused_computation.9.clone.1 | convolution fusion | flops 275513344 | bytes 6449157 | tf_op jit(solution)/shard_map/while/body/eval_jaxpr/dot_general | solution.py:97
  223.9 3.6 fusion.83
  231.0 3.7 %convolution_add_fusion.2 = f32[2048,128]{1,0:T(8,128)} fusion(f32[512,2048]{1,0:T(8,128)S(1)} %copy-done.1, f32[2048]{0:T(1024)S(1)} %ceil_maximum_fusion.2, s32[2048]{0:T(1024)S(1)} %ge.96, s32[512]{0:T(512)S(1)} %bitcast.144, f32[2048,128]{1,0:T(8,128)} %get-tuple-element.306, f32[2048]{0:T(1024)S(1)} %get-tuple-element.291, pred[]{:T(512)S(6)} %compare.3, ...), kind=kOutput, calls=%fused_computation.9.clone.1 | convolution fusion | flops 275513344 | bytes 6449157 | tf_op jit(solution)/shard_map/while/body/eval_jaxpr/dot_general | solution.py:97
  235.0 3.6 fusion.83
  242.0 3.7 %convolution_add_fusion.2 = f32[2048,128]{1,0:T(8,128)} fusion(f32[512,2048]{1,0:T(8,128)S(1)} %copy-done.1, f32[2048]{0:T(1024)S(1)} %ceil_maximum_fusion.2, s32[2048]{0:T(1024)S(1)} %ge.96, s32[512]{0:T(512)S(1)} %bitcast.144, f32[2048,128]{1,0:T(8,128)} %get-tuple-element.306, f32[2048]{0:T(1024)S(1)} %get-tuple-element.291, pred[]{:T(512)S(6)} %compare.3, ...), kind=kOutput, calls=%fused_computation.9.clone.1 | convolution fusion | flops 275513344 | bytes 6449157 | tf_op jit(solution)/shard_map/while/body/eval_jaxpr/dot_general | solution.py:97
  253.1 3.7 %convolution_add_fusion.2 = f32[2048,128]{1,0:T(8,128)} fusion(f32[512,2048]{1,0:T(8,128)S(1)} %copy-done.1, f32[2048]{0:T(1024)S(1)} %ceil_maximum_fusion.2, s32[2048]{0:T(1024)S(1)} %ge.96, s32[512]{0:T(512)S(1)} %bitcast.144, f32[2048,128]{1,0:T(8,128)} %get-tuple-element.306, f32[2048]{0:T(1024)S(1)} %get-tuple-element.291, pred[]{:T(512)S(6)} %compare.3, ...), kind=kOutput, calls=%fused_computation.9.clone.1 | convolution fusion | flops 275513344 | bytes 6449157 | tf_op jit(solution)/shard_map/while/body/eval_jaxpr/dot_general | solution.py:97
  257.0 3.6 fusion.83
  264.1 3.7 %convolution_add_fusion.2 = f32[2048,128]{1,0:T(8,128)} fusion(f32[512,2048]{1,0:T(8,128)S(1)} %copy-done.1, f32[2048]{0:T(1024)S(1)} %ceil_maximum_fusion.2, s32[2048]{0:T(1024)S(1)} %ge.96, s32[512]{0:T(512)S(1)} %bitcast.144, f32[2048,128]{1,0:T(8,128)} %get-tuple-element.306, f32[2048]{0:T(1024)S(1)} %get-tuple-element.291, pred[]{:T(512)S(6)} %compare.3, ...), kind=kOutput, calls=%fused_computation.9.clone.1 | convolution fusion | flops 275513344 | bytes 6449157 | tf_op jit(solution)/shard_map/while/body/eval_jaxpr/dot_general | solution.py:97
  268.1 3.6 fusion.83
  275.2 3.7 %convolution_add_fusion.2 = f32[2048,128]{1,0:T(8,128)} fusion(f32[512,2048]{1,0:T(8,128)S(1)} %copy-done.1, f32[2048]{0:T(1024)S(1)} %ceil_maximum_fusion.2, s32[2048]{0:T(1024)S(1)} %ge.96, s32[512]{0:T(512)S(1)} %bitcast.144, f32[2048,128]{1,0:T(8,128)} %get-tuple-element.306, f32[2048]{0:T(1024)S(1)} %get-tuple-element.291, pred[]{:T(512)S(6)} %compare.3, ...), kind=kOutput, calls=%fused_computation.9.clone.1 | convolution fusion | flops 275513344 | bytes 6449157 | tf_op jit(solution)/shard_map/while/body/eval_jaxpr/dot_general | solution.py:97
  279.1 3.6 fusion.83
  286.2 3.7 %convolution_add_fusion.2 = f32[2048,128]{1,0:T(8,128)} fusion(f32[512,2048]{1,0:T(8,128)S(1)} %copy-done.1, f32[2048]{0:T(1024)S(1)} %ceil_maximum_fusion.2, s32[2048]{0:T(1024)S(1)} %ge.96, s32[512]{0:T(512)S(1)} %bitcast.144, f32[2048,128]{1,0:T(8,128)} %get-tuple-element.306, f32[2048]{0:T(1024)S(1)} %get-tuple-element.291, pred[]{:T(512)S(6)} %compare.3, ...), kind=kOutput, calls=%fused_computation.9.clone.1 | convolution fusion | flops 275513344 | bytes 6449157 | tf_op jit(solution)/shard_map/while/body/eval_jaxpr/dot_general | solution.py:97
  290.2 3.6 fusion.83
  297.3 3.7 %convolution_add_fusion.2 = f32[2048,128]{1,0:T(8,128)} fusion(f32[512,2048]{1,0:T(8,128)S(1)} %copy-done.1, f32[2048]{0:T(1024)S(1)} %ceil_maximum_fusion.2, s32[2048]{0:T(1024)S(1)} %ge.96, s32[512]{0:T(512)S(1)} %bitcast.144, f32[2048,128]{1,0:T(8,128)} %get-tuple-element.306, f32[2048]{0:T(1024)S(1)} %get-tuple-element.291, pred[]{:T(512)S(6)} %compare.3, ...), kind=kOutput, calls=%fused_computation.9.clone.1 | convolution fusion | flops 275513344 | bytes 6449157 | tf_op jit(solution)/shard_map/while/body/eval_jaxpr/dot_general | solution.py:97
  308.3 3.7 %convolution_add_fusion.2 = f32[2048,128]{1,0:T(8,128)} fusion(f32[512,2048]{1,0:T(8,128)S(1)} %copy-done.1, f32[2048]{0:T(1024)S(1)} %ceil_maximum_fusion.2, s32[2048]{0:T(1024)S(1)} %ge.96, s32[512]{0:T(512)S(1)} %bitcast.144, f32[2048,128]{1,0:T(8,128)} %get-tuple-element.306, f32[2048]{0:T(1024)S(1)} %get-tuple-element.291, pred[]{:T(512)S(6)} %compare.3, ...), kind=kOutput, calls=%fused_computation.9.clone.1 | convolution fusion | flops 275513344 | bytes 6449157 | tf_op jit(solution)/shard_map/while/body/eval_jaxpr/dot_general | solution.py:97
  319.4 3.7 %convolution_add_fusion.2 = f32[2048,128]{1,0:T(8,128)} fusion(f32[512,2048]{1,0:T(8,128)S(1)} %copy-done.1, f32[2048]{0:T(1024)S(1)} %ceil_maximum_fusion.2, s32[2048]{0:T(1024)S(1)} %ge.96, s32[512]{0:T(512)S(1)} %bitcast.144, f32[2048,128]{1,0:T(8,128)} %get-tuple-element.306, f32[2048]{0:T(1024)S(1)} %get-tuple-element.291, pred[]{:T(512)S(6)} %compare.3, ...), kind=kOutput, calls=%fused_computation.9.clone.1 | convolution fusion | flops 275513344 | bytes 6449157 | tf_op jit(solution)/shard_map/while/body/eval_jaxpr/dot_general | solution.py:97
  330.4 3.7 %convolution_add_fusion.2 = f32[2048,128]{1,0:T(8,128)} fusion(f32[512,2048]{1,0:T(8,128)S(1)} %copy-done.1, f32[2048]{0:T(1024)S(1)} %ceil_maximum_fusion.2, s32[2048]{0:T(1024)S(1)} %ge.96, s32[512]{0:T(512)S(1)} %bitcast.144, f32[2048,128]{1,0:T(8,128)} %get-tuple-element.306, f32[2048]{0:T(1024)S(1)} %get-tuple-element.291, pred[]{:T(512)S(6)} %compare.3, ...), kind=kOutput, calls=%fused_computation.9.clone.1 | convolution fusion | flops 275513344 | bytes 6449157 | tf_op jit(solution)/shard_map/while/body/eval_jaxpr/dot_general | solution.py:97
  341.5 3.7 %convolution_add_fusion.2 = f32[2048,128]{1,0:T(8,128)} fusion(f32[512,2048]{1,0:T(8,128)S(1)} %copy-done.1, f32[2048]{0:T(1024)S(1)} %ceil_maximum_fusion.2, s32[2048]{0:T(1024)S(1)} %ge.96, s32[512]{0:T(512)S(1)} %bitcast.144, f32[2048,128]{1,0:T(8,128)} %get-tuple-element.306, f32[2048]{0:T(1024)S(1)} %get-tuple-element.291, pred[]{:T(512)S(6)} %compare.3, ...), kind=kOutput, calls=%fused_computation.9.clone.1 | convolution fusion | flops 275513344 | bytes 6449157 | tf_op jit(solution)/shard_map/while/body/eval_jaxpr/dot_general | solution.py:97
  352.5 3.7 %convolution_add_fusion.2 = f32[2048,128]{1,0:T(8,128)} fusion(f32[512,2048]{1,0:T(8,128)S(1)} %copy-done.1, f32[2048]{0:T(1024)S(1)} %ceil_maximum_fusion.2, s32[2048]{0:T(1024)S(1)} %ge.96, s32[512]{0:T(512)S(1)} %bitcast.144, f32[2048,128]{1,0:T(8,128)} %get-tuple-element.306, f32[2048]{0:T(1024)S(1)} %get-tuple-element.291, pred[]{:T(512)S(6)} %compare.3, ...), kind=kOutput, calls=%fused_computation.9.clone.1 | convolution fusion | flops 275513344 | bytes 6449157 | tf_op jit(solution)/shard_map/while/body/eval_jaxpr/dot_general | solution.py:97
  (265 shorter events, 125.3 us)
Async XLA Ops:
  8.0 28.6 %copy-start = (bf16[256,8,128]{2,1,0:T(8,128)(2,1)S(1)}, bf16[256,8,128]{2,1,0:T(8,128)(2,1)}, u32[]{:S(2)}) copy-start(bf16[256,8,128]{2,1,0:T(8,128)(2,1)} %param.21) | copy-start | bytes 1572868
  37.9 15.8 %all-to-all-start.1 = ((f32[32,1,2048]{2,1,0:T(1,128)}), f32[32,1,2048]{2,1,0:T(1,128)S(1)}, u32[]{:S(2)}, u32[]{:S(2)}) async-start(f32[32,1,2048]{2,1,0:T(1,128)} %broadcast_in_dim.109), calls=%async_computation.1 | async-start | bytes 524288 | tf_op jit(solution)/shard_map/all_to_all | solution.py:54
  41.8 50.8 %reduce-scatter.4.cloned.1.call-start = ((), (), s32[]{:S(2)}) async-start(), calls=%async_computation.7 | async-start | bytes 1179648 | tf_op jit(solution)/shard_map/reduce_scatter | solution.py:67
  56.8 35.9 %copy-start.2 = (bf16[256,1,128]{2,0,1:T(8,128)(2,1)S(1)}, bf16[256,1,128]{2,0,1:T(8,128)(2,1)}, u32[]{:S(2)}) copy-start(bf16[256,1,128]{2,0,1:T(8,128)(2,1)} %param.17) | copy-start | bytes 196612
  56.8 35.9 %copy-start.3 = (bf16[256,1,128]{2,0,1:T(8,128)(2,1)S(1)}, bf16[256,1,128]{2,0,1:T(8,128)(2,1)}, u32[]{:S(2)}) copy-start(bf16[256,1,128]{2,0,1:T(8,128)(2,1)} %param.16) | copy-start | bytes 196612
  56.8 36.6 %copy-start.4 = (bf16[128,2,128]{2,1,0:T(2,128)(2,1)S(1)}, bf16[128,2,128]{2,1,0:T(2,128)(2,1)}, u32[]{:S(2)}) copy-start(bf16[128,2,128]{2,1,0:T(2,128)(2,1)} %param.23) | copy-start | bytes 196612
  56.8 36.6 %copy-start.5 = (bf16[128,2,128]{2,1,0:T(2,128)(2,1)S(1)}, bf16[128,2,128]{2,1,0:T(2,128)(2,1)}, u32[]{:S(2)}) copy-start(bf16[128,2,128]{2,1,0:T(2,128)(2,1)} %param.22) | copy-start | bytes 196612
  56.9 41.2 %copy-start.8 = (s32[256]{0:T(256)S(1)}, s32[256]{0:T(256)}, u32[]{:S(2)}) copy-start(s32[256]{0:T(256)} %param.24) | copy-start | bytes 3076
  58.4 94.8 %reduce-scatter.8.cloned.1.call-start = ((), (), s32[]{:S(2)}) async-start(), calls=%async_computation.9 | async-start | bytes 147456 | tf_op jit(solution)/shard_map/reduce_scatter | solution.py:67
  59.2 111.2 %reduce-scatter.6.cloned.1.call-start = ((), (), s32[]{:S(2)}) async-start(), calls=%async_computation.8 | async-start | bytes 163840 | tf_op jit(solution)/shard_map/reduce_scatter | solution.py:67
  92.7 84.2 %all-gather.3.cloned.1.call-start = ((), (), s32[]{:S(2)}) async-start(), calls=%async_computation.6 | async-start | bytes 4325376 | tf_op jit(solution)/shard_map/all_gather | solution.py:18
  94.2 52.0 %all-to-all-start.2 = ((bf16[128,2,256]{2,0,1:T(8,128)(2,1)}), bf16[128,2,256]{2,0,1:T(8,128)(2,1)S(1)}, u32[]{:S(2)}, u32[]{:S(2)}) async-start(bf16[128,2,256]{2,0,1:T(8,128)(2,1)} %pad_maximum_fusion.1), calls=%async_computation.4 | async-start | bytes 262144 | tf_op jit(solution)/shard_map/all_to_all | solution.py:45
  99.5 2.3 copy-start.6
  100.3 44.6 %copy-start.9 = (u32[256]{0:T(256)S(1)}, u32[256]{0:T(256)}, u32[]{:S(2)}) copy-start(u32[256]{0:T(256)} %constant.138) | copy-start | bytes 3076
  171.9 8.8 %copy-start.7 = (bf16[256,8,128]{2,1,0:T(8,128)(2,1)S(1)}, bf16[256,8,128]{2,1,0:T(8,128)(2,1)}, u32[]{:S(2)}) copy-start(bf16[256,8,128]{2,1,0:T(8,128)(2,1)} %param.15) | copy-start | bytes 1572868
  184.5 3.5 copy-start.1
  194.3 3.5 copy-start.1
  205.4 3.5 copy-start.1
  216.4 3.5 copy-start.1
  227.5 3.5 copy-start.1
  238.5 3.5 copy-start.1
  249.6 3.5 copy-start.1
  260.6 3.5 copy-start.1
  271.7 3.5 copy-start.1
  282.7 3.5 copy-start.1
  293.8 3.5 copy-start.1
  304.8 3.5 copy-start.1
  315.9 3.5 copy-start.1
  326.9 3.5 copy-start.1
  338.0 3.5 copy-start.1
  349.0 3.5 copy-start.1
Sparse Core Ops, SparseCore 0:
  58.5 34.1 reduce-scatter.3
  95.1 35.5 reduce-scatter.7
  133.3 27.6 reduce-scatter.5
Sparse Core Ops, SparseCore 1:
  96.3 80.5 all-gather.2
where the time goes:
time: 367 us; the launch traced here: 366 us
  matrix products  122 us (33%)
  blocking collectives  80.6 us (22%)
  other arithmetic  69.4 us (19%)
  waiting for transfers between devices  50.3 us (14%)
  local copies, waits for them, and re-layouts  18.5 us (5%)
  between operations  16.4 us (4%)
  starting transfers between devices  7.94 us (2%)
    dot_general x16, matrix products, online_step(): jnp.dot(weights.astype(jnp.bfloat16), value_block, preferred_element_type...  58.4 us
    dot_general x16, matrix products, attend(): jnp.einsum('qd,kd->qk', query_rows, key_block, preferred_element_type=jnp...  57.2 us
    reduce_sum x16, other arithmetic, online_step(): new_mass = old_mass * factor + jnp.sum(weights, axis=1)  55.4 us
    all_gather x1, blocking collectives, body(): lax.all_gather(token_pos, CTX, axis=0, tiled=True)  42.4 us
    reduce_scatter x3, waiting for transfers between devices, summed_rows(): nearer = lax.psum_scatter(array, axes[0], scatter_dimension=dim, tiled=True)  33.4 us
    all_to_all x1, blocking collectives, sent_together(): lax.all_to_all(both, axis, split_axis=split_dim, concat_axis=concat_dim,...  21.9 us
    unnamed x1, blocking collectives  16.3 us
    all_to_all x1, waiting for transfers between devices, sent_to_all(): lax.all_to_all(jnp.broadcast_to(array[None], (devices, *array.shape)), ax...  11.8 us
  transfers between devices with their start and end apart: 6, of which 3 were waited for; matrix products, arithmetic and copies ran while one was open for 4% of the time, Pallas kernels for 0%

commit v1 on v0

--- a/solution.py
+++ b/solution.py
@@ -10,6 +10,13 @@
 NEG_FILL = -1e30
 FP_LIMIT = 448.0
 LOG_TWO_E = 1.4426950408889634
+
+
+def mark_trails_on(local_block):
+    outer = jnp.stack([local_block for _ in range(lax.axis_size(CTX))])
+    new = lax.all_to_all(outer, axis_name=CTX, split_axis=0, concat_axis=0)
+    state_next = jnp.concatenate(new, axis=0)
+    return state_next
 
 
 def side_by_side(arrays, axis, dim, along):
@@ -138,7 +145,7 @@
     running = start_state
     key_piece, value_piece, place_piece = (
         *side_by_side((local_keys, local_values), CTX, 0, 1),
-        lax.all_gather(token_pos, CTX, axis=0, tiled=True),
+        mark_trails_on(token_pos),
     )
     row_count = key_piece.shape[0]
     block_rows = math.gcd(row_count, 512)

time: 367 us -> 367 us (level)
  blocking collectives: 80.6 us -> 39.6 us
  waiting for transfers between devices: 50.3 us -> 83.6 us
  starting transfers between devices: 7.94 us -> 15.1 us
    all_gather x1 -> x0, blocking collectives: 42.4 us -> none  [body(): lax.all_gather(token_pos, CTX, axis=0, tiled=True)]
    reduce_scatter x3, waiting for transfers between devices: 33.4 us -> 51.4 us  [summed_rows(): nearer = lax.psum_scatter(array, axes[0], scatter_dimension=dim, tiled=True)]
    all_gather x1, waiting for transfers between devices: 5.02 us -> 14.5 us  [side_by_side(): whole = lax.all_gather(both, axis, axis=dim, tiled=True)]
    all_to_all x0 -> x1, starting transfers between devices: none -> 7.16 us  [mark_trails_on(): new = lax.all_to_all(outer, axis_name=CTX, split_axis=0, concat_axis=0)]
    all_to_all x0 -> x1, waiting for transfers between devices: none -> 5.69 us  [mark_trails_on(): new = lax.all_to_all(outer, axis_name=CTX, split_axis=0, concat_axis=0)]
  transfers between devices with their start and end apart: 6 -> 7, of which waited for: 3 -> 7; matrix products, arithmetic and copies ran while one was open for 4% -> 5% of each run, Pallas kernels for 0% -> 0%
where the time goes in v1:
time: 367 us; the launch traced here: 366 us
  matrix products  122 us (33%)
  waiting for transfers between devices  83.6 us (23%)
  other arithmetic  69.4 us (19%)
  blocking collectives  39.6 us (11%)
  local copies, waits for them, and re-layouts  19.1 us (5%)
  between operations  16.4 us (4%)
  starting transfers between devices  15.1 us (4%)
    dot_general x16, matrix products, online_step(): jnp.dot(weights.astype(jnp.bfloat16), value_block, preferred_element_type...  58.4 us
    dot_general x16, matrix products, attend(): jnp.einsum('qd,kd->qk', query_rows, key_block, preferred_element_type=jnp...  57.2 us
    reduce_sum x16, other arithmetic, online_step(): new_mass = old_mass * factor + jnp.sum(weights, axis=1)  55.4 us
    reduce_scatter x3, waiting for transfers between devices, summed_rows(): nearer = lax.psum_scatter(array, axes[0], scatter_dimension=dim, tiled=True)  51.4 us
    all_to_all x1, blocking collectives, sent_together(): lax.all_to_all(both, axis, split_axis=split_dim, concat_axis=concat_dim,...  21.9 us
    unnamed x1, blocking collectives  17.6 us
    all_gather x1, waiting for transfers between devices, side_by_side(): whole = lax.all_gather(both, axis, axis=dim, tiled=True)  14.5 us
    all_to_all x1, waiting for transfers between devices, sent_to_all(): lax.all_to_all(jnp.broadcast_to(array[None], (devices, *array.shape)), ax...  11.8 us
  transfers between devices with their start and end apart: 7, of which 7 were waited for; matrix products, arithmetic and copies ran while one was open for 5% of the time, Pallas kernels for 0%

profile of v1, /device:TPU:8, one launch (start us, length us, event | category | flops | bytes accessed | tf_op | source)
XLA Modules:
  0.0 365.8 jit_solution(16928065230971751439)
XLA Ops:
  14.2 21.9 %all_to_all.42 = bf16[32,2,1025]{2,1,0:T(2,128)(2,1)S(1)} all-to-all(bf16[32,2,1025]{2,1,0:T(2,128)(2,1)S(1)} %reshape.284), channel_id=1, replica_groups=mesh['ctx_0'=8,'ctx_1'=4,'head'=4,'side'=2] {'ctx_0','ctx_1'}, dimensions={0} | all-to-all | bytes 262400 | tf_op jit(solution)/shard_map/all_to_all | solution.py:33
  37.9 3.9 %all-to-all-start.2 = ((f32[32,1,2048]{2,1,0:T(1,128)}), f32[32,1,2048]{2,1,0:T(1,128)S(1)}, u32[]{:S(2)}, u32[]{:S(2)}) async-start(f32[32,1,2048]{2,1,0:T(1,128)} %broadcast_in_dim.109), calls=%async_computation.2 | async-start | bytes 524288 | tf_op jit(solution)/shard_map/all_to_all | solution.py:61
  41.9 11.8 %all-to-all-done.2 = f32[32,1,2048]{2,1,0:T(1,128)S(1)} async-done(((f32[32,1,2048]{2,1,0:T(1,128)}), f32[32,1,2048]{2,1,0:T(1,128)S(1)}, u32[]{:S(2)}, u32[]{:S(2)}) %all-to-all-start.2) | async-done | bytes 262176 | tf_op jit(solution)/shard_map/all_to_all | solution.py:61
  59.3 33.5 %reduce-scatter.4.cloned.1.call-done = f32[32,8,128]{2,0,1:T(8,128)} async-done(((f32[256,8,128]{2,0,1:T(8,128)}), f32[32,8,128]{2,0,1:T(8,128)}) %reduce-scatter.4.cloned.1.call-update) | async-done | bytes 131088 | tf_op jit(solution)/shard_map/reduce_scatter | solution.py:74
  94.2 7.2 %all-to-all-start = ((s32[32,1,256]{2,1,0:T(1,128)}), s32[32,1,256]{2,1,0:T(1,128)S(1)}, u32[]{:S(2)}, u32[]{:S(2)}) async-start(s32[32,1,256]{2,1,0:T(1,128)} %stack.2), calls=%async_computation | async-start | bytes 65536 | tf_op jit(solution)/shard_map/all_to_all | solution.py:17
  105.5 5.7 %all-to-all-done = s32[32,1,256]{2,1,0:T(1,128)S(1)} async-done(((s32[32,1,256]{2,1,0:T(1,128)}), s32[32,1,256]{2,1,0:T(1,128)S(1)}, u32[]{:S(2)}, u32[]{:S(2)}) %all-to-all-start) | async-done | bytes 32800 | tf_op jit(solution)/shard_map/all_to_all | solution.py:17
  111.2 3.9 %all-to-all-start.3 = ((bf16[128,2,256]{2,0,1:T(8,128)(2,1)}), bf16[128,2,256]{2,0,1:T(8,128)(2,1)S(1)}, u32[]{:S(2)}, u32[]{:S(2)}) async-start(bf16[128,2,256]{2,0,1:T(8,128)(2,1)} %pad_maximum_fusion.1), calls=%async_computation.5 | async-start | bytes 262144 | tf_op jit(solution)/shard_map/all_to_all | solution.py:52
  124.5 6.3 %reduce-scatter.8.cloned.1.call-done = f32[32,8]{1,0:T(8,128)} async-done(((f32[256,8]{1,0:T(8,128)}), f32[32,8]{1,0:T(8,128)}) %reduce-scatter.8.cloned.1.call-update) | async-done | bytes 1040 | tf_op jit(solution)/shard_map/reduce_scatter | solution.py:74
  130.9 17.6 %all-reduce = f32[32,8]{1,0:T(8,128)S(1)} all-reduce(f32[32,8]{1,0:T(8,128)} %reduce-scatter.8.cloned.1.call-done), channel_id=5, replica_groups=mesh['ctx_0'=8,'ctx_1'=4,'head'=4,'side'=2] {'ctx_1'}, use_global_device_ids=true, to_apply=%region_13.15.clone | all-reduce | flops 256 | bytes 2048
  149.4 11.6 %reduce-scatter.6.cloned.1.call-done = f32[8,8,128]{2,0,1:T(8,128)} async-done(((f32[32,8,128]{2,0,1:T(8,128)}), f32[8,8,128]{2,0,1:T(8,128)}) %reduce-scatter.6.cloned.1.call-update) | async-done | bytes 32784 | tf_op jit(solution)/shard_map/reduce_scatter | solution.py:74
  162.5 14.5 %all-gather.2.cloned.1.call-done = bf16[8192,256]{1,0:T(8,128)(2,1)} async-done(((bf16[256,256]{1,0:T(8,128)(2,1)}), bf16[8192,256]{1,0:T(8,128)(2,1)}) %all-gather.2.cloned.1.call-update) | async-done | bytes 4194320 | tf_op jit(solution)/shard_map/all_gather | solution.py:25
  176.9 3.8 %fusion.54 = (bf16[8192,128]{1,0:T(8,128)(2,1)S(1)}, bf16[8192,128]{1,0:T(8,128)(2,1)}) fusion(bf16[8192,256]{1,0:T(8,128)(2,1)} %all-gather.2.cloned.1.call-done), kind=kLoop, calls=%fused_computation.116 | loop fusion | bytes 8388608 | tf_op jit(solution)/shard_map/split | solution.py:26
  180.7 175.6 %while.17 = (s32[]{:T(128)}, f32[2048]{0:T(1024)S(1)}, f32[2048]{0:T(1024)S(1)}, f32[2048,128]{1,0:T(8,128)}, s32[16,512]{1,0:T(8,128)S(1)}, /*index=5*/bf16[16,...) while((s32[]{:T(128)}, f32[2048]{0:T(1024)S(1)}, ...), condition=%wide.region_3.4_spmd.clone, body=%wide.region_0.3_spmd.clone.sunk | while | flops 554450944 | bytes 32435368 | solution.py:157
  190.8 3.6 fusion.83
  197.9 3.7 %convolution_add_fusion.2 = f32[2048,128]{1,0:T(8,128)} fusion(f32[512,2048]{1,0:T(8,128)S(1)} %copy-done.1, f32[2048]{0:T(1024)S(1)} %ceil_maximum_fusion.2, s32[2048]{0:T(1024)S(1)} %ge.96, s32[512]{0:T(512)S(1)} %bitcast.143, f32[2048,128]{1,0:T(8,128)} %get-tuple-element.306, f32[2048]{0:T(1024)S(1)} %get-tuple-element.291, pred[]{:T(512)S(6)} %compare.3, ...), kind=kOutput, calls=%fused_computation.9.clone.1 | convolution fusion | flops 275513344 | bytes 6449157 | tf_op jit(solution)/shard_map/while/body/eval_jaxpr/dot_general | solution.py:104
  201.9 3.6 fusion.83
  208.9 3.7 %convolution_add_fusion.2 = f32[2048,128]{1,0:T(8,128)} fusion(f32[512,2048]{1,0:T(8,128)S(1)} %copy-done.1, f32[2048]{0:T(1024)S(1)} %ceil_maximum_fusion.2, s32[2048]{0:T(1024)S(1)} %ge.96, s32[512]{0:T(512)S(1)} %bitcast.143, f32[2048,128]{1,0:T(8,128)} %get-tuple-element.306, f32[2048]{0:T(1024)S(1)} %get-tuple-element.291, pred[]{:T(512)S(6)} %compare.3, ...), kind=kOutput, calls=%fused_computation.9.clone.1 | convolution fusion | flops 275513344 | bytes 6449157 | tf_op jit(solution)/shard_map/while/body/eval_jaxpr/dot_general | solution.py:104
  212.9 3.6 fusion.83
  220.0 3.7 %convolution_add_fusion.2 = f32[2048,128]{1,0:T(8,128)} fusion(f32[512,2048]{1,0:T(8,128)S(1)} %copy-done.1, f32[2048]{0:T(1024)S(1)} %ceil_maximum_fusion.2, s32[2048]{0:T(1024)S(1)} %ge.96, s32[512]{0:T(512)S(1)} %bitcast.143, f32[2048,128]{1,0:T(8,128)} %get-tuple-element.306, f32[2048]{0:T(1024)S(1)} %get-tuple-element.291, pred[]{:T(512)S(6)} %compare.3, ...), kind=kOutput, calls=%fused_computation.9.clone.1 | convolution fusion | flops 275513344 | bytes 6449157 | tf_op jit(solution)/shard_map/while/body/eval_jaxpr/dot_general | solution.py:104
  224.0 3.6 fusion.83
  231.0 3.7 %convolution_add_fusion.2 = f32[2048,128]{1,0:T(8,128)} fusion(f32[512,2048]{1,0:T(8,128)S(1)} %copy-done.1, f32[2048]{0:T(1024)S(1)} %ceil_maximum_fusion.2, s32[2048]{0:T(1024)S(1)} %ge.96, s32[512]{0:T(512)S(1)} %bitcast.143, f32[2048,128]{1,0:T(8,128)} %get-tuple-element.306, f32[2048]{0:T(1024)S(1)} %get-tuple-element.291, pred[]{:T(512)S(6)} %compare.3, ...), kind=kOutput, calls=%fused_computation.9.clone.1 | convolution fusion | flops 275513344 | bytes 6449157 | tf_op jit(solution)/shard_map/while/body/eval_jaxpr/dot_general | solution.py:104
  242.1 3.7 %convolution_add_fusion.2 = f32[2048,128]{1,0:T(8,128)} fusion(f32[512,2048]{1,0:T(8,128)S(1)} %copy-done.1, f32[2048]{0:T(1024)S(1)} %ceil_maximum_fusion.2, s32[2048]{0:T(1024)S(1)} %ge.96, s32[512]{0:T(512)S(1)} %bitcast.143, f32[2048,128]{1,0:T(8,128)} %get-tuple-element.306, f32[2048]{0:T(1024)S(1)} %get-tuple-element.291, pred[]{:T(512)S(6)} %compare.3, ...), kind=kOutput, calls=%fused_computation.9.clone.1 | convolution fusion | flops 275513344 | bytes 6449157 | tf_op jit(solution)/shard_map/while/body/eval_jaxpr/dot_general | solution.py:104
  253.1 3.7 %convolution_add_fusion.2 = f32[2048,128]{1,0:T(8,128)} fusion(f32[512,2048]{1,0:T(8,128)S(1)} %copy-done.1, f32[2048]{0:T(1024)S(1)} %ceil_maximum_fusion.2, s32[2048]{0:T(1024)S(1)} %ge.96, s32[512]{0:T(512)S(1)} %bitcast.143, f32[2048,128]{1,0:T(8,128)} %get-tuple-element.306, f32[2048]{0:T(1024)S(1)} %get-tuple-element.291, pred[]{:T(512)S(6)} %compare.3, ...), kind=kOutput, calls=%fused_computation.9.clone.1 | convolution fusion | flops 275513344 | bytes 6449157 | tf_op jit(solution)/shard_map/while/body/eval_jaxpr/dot_general | solution.py:104
  264.2 3.7 %convolution_add_fusion.2 = f32[2048,128]{1,0:T(8,128)} fusion(f32[512,2048]{1,0:T(8,128)S(1)} %copy-done.1, f32[2048]{0:T(1024)S(1)} %ceil_maximum_fusion.2, s32[2048]{0:T(1024)S(1)} %ge.96, s32[512]{0:T(512)S(1)} %bitcast.143, f32[2048,128]{1,0:T(8,128)} %get-tuple-element.306, f32[2048]{0:T(1024)S(1)} %get-tuple-element.291, pred[]{:T(512)S(6)} %compare.3, ...), kind=kOutput, calls=%fused_computation.9.clone.1 | convolution fusion | flops 275513344 | bytes 6449157 | tf_op jit(solution)/shard_map/while/body/eval_jaxpr/dot_general | solution.py:104
  275.2 3.7 %convolution_add_fusion.2 = f32[2048,128]{1,0:T(8,128)} fusion(f32[512,2048]{1,0:T(8,128)S(1)} %copy-done.1, f32[2048]{0:T(1024)S(1)} %ceil_maximum_fusion.2, s32[2048]{0:T(1024)S(1)} %ge.96, s32[512]{0:T(512)S(1)} %bitcast.143, f32[2048,128]{1,0:T(8,128)} %get-tuple-element.306, f32[2048]{0:T(1024)S(1)} %get-tuple-element.291, pred[]{:T(512)S(6)} %compare.3, ...), kind=kOutput, calls=%fused_computation.9.clone.1 | convolution fusion | flops 275513344 | bytes 6449157 | tf_op jit(solution)/shard_map/while/body/eval_jaxpr/dot_general | solution.py:104
  286.3 3.7 %convolution_add_fusion.2 = f32[2048,128]{1,0:T(8,128)} fusion(f32[512,2048]{1,0:T(8,128)S(1)} %copy-done.1, f32[2048]{0:T(1024)S(1)} %ceil_maximum_fusion.2, s32[2048]{0:T(1024)S(1)} %ge.96, s32[512]{0:T(512)S(1)} %bitcast.143, f32[2048,128]{1,0:T(8,128)} %get-tuple-element.306, f32[2048]{0:T(1024)S(1)} %get-tuple-element.291, pred[]{:T(512)S(6)} %compare.3, ...), kind=kOutput, calls=%fused_computation.9.clone.1 | convolution fusion | flops 275513344 | bytes 6449157 | tf_op jit(solution)/shard_map/while/body/eval_jaxpr/dot_general | solution.py:104
  297.3 3.7 %convolution_add_fusion.2 = f32[2048,128]{1,0:T(8,128)} fusion(f32[512,2048]{1,0:T(8,128)S(1)} %copy-done.1, f32[2048]{0:T(1024)S(1)} %ceil_maximum_fusion.2, s32[2048]{0:T(1024)S(1)} %ge.96, s32[512]{0:T(512)S(1)} %bitcast.143, f32[2048,128]{1,0:T(8,128)} %get-tuple-element.306, f32[2048]{0:T(1024)S(1)} %get-tuple-element.291, pred[]{:T(512)S(6)} %compare.3, ...), kind=kOutput, calls=%fused_computation.9.clone.1 | convolution fusion | flops 275513344 | bytes 6449157 | tf_op jit(solution)/shard_map/while/body/eval_jaxpr/dot_general | solution.py:104
  308.4 3.7 %convolution_add_fusion.2 = f32[2048,128]{1,0:T(8,128)} fusion(f32[512,2048]{1,0:T(8,128)S(1)} %copy-done.1, f32[2048]{0:T(1024)S(1)} %ceil_maximum_fusion.2, s32[2048]{0:T(1024)S(1)} %ge.96, s32[512]{0:T(512)S(1)} %bitcast.143, f32[2048,128]{1,0:T(8,128)} %get-tuple-element.306, f32[2048]{0:T(1024)S(1)} %get-tuple-element.291, pred[]{:T(512)S(6)} %compare.3, ...), kind=kOutput, calls=%fused_computation.9.clone.1 | convolution fusion | flops 275513344 | bytes 6449157 | tf_op jit(solution)/shard_map/while/body/eval_jaxpr/dot_general | solution.py:104
  319.4 3.7 %convolution_add_fusion.2 = f32[2048,128]{1,0:T(8,128)} fusion(f32[512,2048]{1,0:T(8,128)S(1)} %copy-done.1, f32[2048]{0:T(1024)S(1)} %ceil_maximum_fusion.2, s32[2048]{0:T(1024)S(1)} %ge.96, s32[512]{0:T(512)S(1)} %bitcast.143, f32[2048,128]{1,0:T(8,128)} %get-tuple-element.306, f32[2048]{0:T(1024)S(1)} %get-tuple-element.291, pred[]{:T(512)S(6)} %compare.3, ...), kind=kOutput, calls=%fused_computation.9.clone.1 | convolution fusion | flops 275513344 | bytes 6449157 | tf_op jit(solution)/shard_map/while/body/eval_jaxpr/dot_general | solution.py:104
  330.5 3.7 %convolution_add_fusion.2 = f32[2048,128]{1,0:T(8,128)} fusion(f32[512,2048]{1,0:T(8,128)S(1)} %copy-done.1, f32[2048]{0:T(1024)S(1)} %ceil_maximum_fusion.2, s32[2048]{0:T(1024)S(1)} %ge.96, s32[512]{0:T(512)S(1)} %bitcast.143, f32[2048,128]{1,0:T(8,128)} %get-tuple-element.306, f32[2048]{0:T(1024)S(1)} %get-tuple-element.291, pred[]{:T(512)S(6)} %compare.3, ...), kind=kOutput, calls=%fused_computation.9.clone.1 | convolution fusion | flops 275513344 | bytes 6449157 | tf_op jit(solution)/shard_map/while/body/eval_jaxpr/dot_general | solution.py:104
  341.5 3.7 %convolution_add_fusion.2 = f32[2048,128]{1,0:T(8,128)} fusion(f32[512,2048]{1,0:T(8,128)S(1)} %copy-done.1, f32[2048]{0:T(1024)S(1)} %ceil_maximum_fusion.2, s32[2048]{0:T(1024)S(1)} %ge.96, s32[512]{0:T(512)S(1)} %bitcast.143, f32[2048,128]{1,0:T(8,128)} %get-tuple-element.306, f32[2048]{0:T(1024)S(1)} %get-tuple-element.291, pred[]{:T(512)S(6)} %compare.3, ...), kind=kOutput, calls=%fused_computation.9.clone.1 | convolution fusion | flops 275513344 | bytes 6449157 | tf_op jit(solution)/shard_map/while/body/eval_jaxpr/dot_general | solution.py:104
  352.6 3.7 %convolution_add_fusion.2 = f32[2048,128]{1,0:T(8,128)} fusion(f32[512,2048]{1,0:T(8,128)S(1)} %copy-done.1, f32[2048]{0:T(1024)S(1)} %ceil_maximum_fusion.2, s32[2048]{0:T(1024)S(1)} %ge.96, s32[512]{0:T(512)S(1)} %bitcast.143, f32[2048,128]{1,0:T(8,128)} %get-tuple-element.306, f32[2048]{0:T(1024)S(1)} %get-tuple-element.291, pred[]{:T(512)S(6)} %compare.3, ...), kind=kOutput, calls=%fused_computation.9.clone.1 | convolution fusion | flops 275513344 | bytes 6449157 | tf_op jit(solution)/shard_map/while/body/eval_jaxpr/dot_general | solution.py:104
  (267 shorter events, 136.8 us)
Async XLA Ops:
  8.0 28.6 %copy-start = (bf16[256,8,128]{2,1,0:T(8,128)(2,1)S(1)}, bf16[256,8,128]{2,1,0:T(8,128)(2,1)}, u32[]{:S(2)}) copy-start(bf16[256,8,128]{2,1,0:T(8,128)(2,1)} %param.21) | copy-start | bytes 1572868
  37.9 15.8 %all-to-all-start.2 = ((f32[32,1,2048]{2,1,0:T(1,128)}), f32[32,1,2048]{2,1,0:T(1,128)S(1)}, u32[]{:S(2)}, u32[]{:S(2)}) async-start(f32[32,1,2048]{2,1,0:T(1,128)} %broadcast_in_dim.109), calls=%async_computation.2 | async-start | bytes 524288 | tf_op jit(solution)/shard_map/all_to_all | solution.py:61
  41.8 50.9 %reduce-scatter.4.cloned.1.call-start = ((), (), s32[]{:S(2)}) async-start(), calls=%async_computation.8 | async-start | bytes 1179648 | tf_op jit(solution)/shard_map/reduce_scatter | solution.py:74
  56.8 36.0 %copy-start.2 = (bf16[256,1,128]{2,0,1:T(8,128)(2,1)S(1)}, bf16[256,1,128]{2,0,1:T(8,128)(2,1)}, u32[]{:S(2)}) copy-start(bf16[256,1,128]{2,0,1:T(8,128)(2,1)} %param.17) | copy-start | bytes 196612
  56.8 36.0 %copy-start.3 = (bf16[256,1,128]{2,0,1:T(8,128)(2,1)S(1)}, bf16[256,1,128]{2,0,1:T(8,128)(2,1)}, u32[]{:S(2)}) copy-start(bf16[256,1,128]{2,0,1:T(8,128)(2,1)} %param.16) | copy-start | bytes 196612
  56.8 36.7 %copy-start.6 = (s32[256]{0:T(256)S(1)}, s32[256]{0:T(256)}, u32[]{:S(2)}) copy-start(s32[256]{0:T(256)} %param.18) | copy-start | bytes 3076
  56.8 44.5 %copy-start.4 = (bf16[128,2,128]{2,1,0:T(2,128)(2,1)S(1)}, bf16[128,2,128]{2,1,0:T(2,128)(2,1)}, u32[]{:S(2)}) copy-start(bf16[128,2,128]{2,1,0:T(2,128)(2,1)} %param.23) | copy-start | bytes 196612
  56.9 44.5 %copy-start.5 = (bf16[128,2,128]{2,1,0:T(2,128)(2,1)S(1)}, bf16[128,2,128]{2,1,0:T(2,128)(2,1)}, u32[]{:S(2)}) copy-start(bf16[128,2,128]{2,1,0:T(2,128)(2,1)} %param.22) | copy-start | bytes 196612
  56.9 44.5 %copy-start.8 = (s32[256]{0:T(256)S(1)}, s32[256]{0:T(256)}, u32[]{:S(2)}) copy-start(s32[256]{0:T(256)} %param.24) | copy-start | bytes 3076
  58.4 72.5 %reduce-scatter.8.cloned.1.call-start = ((), (), s32[]{:S(2)}) async-start(), calls=%async_computation.10 | async-start | bytes 147456 | tf_op jit(solution)/shard_map/reduce_scatter | solution.py:74
  59.2 101.8 %reduce-scatter.6.cloned.1.call-start = ((), (), s32[]{:S(2)}) async-start(), calls=%async_computation.9 | async-start | bytes 163840 | tf_op jit(solution)/shard_map/reduce_scatter | solution.py:74
  92.7 84.2 %all-gather.2.cloned.1.call-start = ((), (), s32[]{:S(2)}) async-start(), calls=%async_computation.7 | async-start | bytes 4325376 | tf_op jit(solution)/shard_map/all_gather | solution.py:25
  94.2 17.0 %all-to-all-start = ((s32[32,1,256]{2,1,0:T(1,128)}), s32[32,1,256]{2,1,0:T(1,128)S(1)}, u32[]{:S(2)}, u32[]{:S(2)}) async-start(s32[32,1,256]{2,1,0:T(1,128)} %stack.2), calls=%async_computation | async-start | bytes 65536 | tf_op jit(solution)/shard_map/all_to_all | solution.py:17
  103.6 12.4 %copy-start.9 = (u32[256]{0:T(256)S(1)}, u32[256]{0:T(256)}, u32[]{:S(2)}) copy-start(u32[256]{0:T(256)} %constant.138) | copy-start | bytes 3076
  111.2 6.4 %all-to-all-start.3 = ((bf16[128,2,256]{2,0,1:T(8,128)(2,1)}), bf16[128,2,256]{2,0,1:T(8,128)(2,1)S(1)}, u32[]{:S(2)}, u32[]{:S(2)}) async-start(bf16[128,2,256]{2,0,1:T(8,128)(2,1)} %pad_maximum_fusion.1), calls=%async_computation.5 | async-start | bytes 262144 | tf_op jit(solution)/shard_map/all_to_all | solution.py:52
  162.5 18.3 %copy-start.7 = (bf16[256,8,128]{2,1,0:T(8,128)(2,1)S(1)}, bf16[256,8,128]{2,1,0:T(8,128)(2,1)}, u32[]{:S(2)}) copy-start(bf16[256,8,128]{2,1,0:T(8,128)(2,1)} %param.15) | copy-start | bytes 1572868
  184.6 3.5 copy-start.1
  194.4 3.5 copy-start.1
  205.4 3.5 copy-start.1
  216.5 3.5 copy-start.1
  227.5 3.5 copy-start.1
  238.6 3.5 copy-start.1
  249.6 3.5 copy-start.1
  260.7 3.5 copy-start.1
  271.7 3.5 copy-start.1
  282.8 3.5 copy-start.1
  293.8 3.5 copy-start.1
  304.9 3.5 copy-start.1
  315.9 3.5 copy-start.1
  327.0 3.5 copy-start.1
  338.0 3.5 copy-start.1
  349.1 3.5 copy-start.1
Sparse Core Ops, SparseCore 0:
  58.5 34.1 reduce-scatter.3
  95.2 35.5 reduce-scatter.7
  133.4 27.5 reduce-scatter.5
Sparse Core Ops, SparseCore 1:
  96.4 80.5 all-gather.1
